TPU v7x, 256 devices: a whole 4x4x8 slice. The times are simulated.
256 devices in a mesh: replica: 8 (over x_hi, y), shard: 32 (over z, x_lo, core).
Axes of the slice: x: 4 (x_hi: 2, x_lo: 2; x = x_hi * 2 + x_lo), y: 4, z: 8, core: 2. Of those that a mesh axis runs over, the one named last changes fastest.
Arguments:
- master_weight: float32 [32, 1024, 4096], P(None, 'replica', 'shard'), may hold values from -0.1875 to 0.1875
- gradient: bfloat16 [32, 1024, 4096], P(None, 'replica', 'shard'), may hold values from -6 to 6
- first_moment: bfloat16 [32, 1024, 4096], P(None, 'replica', 'shard'), may hold values from -1.796875 to 1.796875
- second_moment: bfloat16 [32, 1024, 4096], P(None, 'replica', 'shard'), may hold values from 0.049804688 to 2
- hidden: bfloat16 [8, 32, 384, 1024], P('replica', 'shard'), may hold values from -6 to 6
- owner_of_expert: int32 [32], replicated, may hold values from 0 to 31, each once
- slab_order: int32 [8], replicated, may hold values from 0 to 7, each once
Outputs:
- new_master: float32 [32, 1024, 4096], P(None, 'replica', 'shard')
- new_first: bfloat16 [32, 1024, 4096], P(None, 'replica', 'shard')
- new_second: bfloat16 [32, 1024, 4096], P(None, 'replica', 'shard')
- expert_out: bfloat16 [8, 32, 384, 4096], P('replica', 'shard')
Inputs may be any that keep to these rules, and one draw needn't show every extreme that they name: `owner_of_expert`: a permutation: every owner holds exactly one expert. A permutation: row slab j of the learner's arrays holds hidden units from slab_order[j] * 128 on.
All inputs are finite; a program needn't handle non-finite values.
Results may differ from a plain program's by a relative error of at most 0.0049.
Values may be sent and summed in bfloat16 or wider, within the bound.
A program may use at most 128 MiB of HBM per device.

v0:
```python
import jax
import jax.numpy as jnp
from jax import lax
from jax.sharding import PartitionSpec as P

D = 4096
QB = 128


beta_one = 0.9
beta_two = 0.95
learn_rate = 0.004
adam_epsilon = 1e-08
step_count = 10.0
quant_limit = 448.0
scale_epsilon = 1e-06


def adam_step(master_weight, gradient, first_moment, second_moment):
    float_gradient = gradient.astype(jnp.float32)
    moment_one = beta_one * first_moment.astype(jnp.float32) + (1.0 - beta_one) * float_gradient
    moment_two = (
        beta_two * second_moment.astype(jnp.float32)
        + (1.0 - beta_two) * float_gradient * float_gradient
    )
    first_fix = 1.0 - beta_one**step_count
    second_fix = 1.0 - beta_two**step_count
    update = moment_one / first_fix / (jnp.sqrt(moment_two / second_fix) + adam_epsilon)
    return (master_weight - learn_rate * update, moment_one, moment_two)


def quantize(weights):
    number, height, breadth = weights.shape
    blocks = weights.reshape(number, height // QB, QB, breadth // QB, QB)
    largest = jnp.max(jnp.abs(blocks), axis=(2, 4))
    block_scale = ((largest + scale_epsilon) / quant_limit).astype(jnp.bfloat16)
    block_scale = lax.optimization_barrier(block_scale)
    divided = blocks / block_scale.astype(jnp.float32)[:, :, None, :, None]
    return (divided.astype(jnp.bfloat16).reshape(number, height, breadth), block_scale)


def scaled_product(summed, left_part, quant_rows, scale_rows):
    token_count = left_part.shape[0]
    breadth = quant_rows.shape[1]
    partial_value = jnp.dot(left_part, quant_rows, preferred_element_type=jnp.float32)
    factor = scale_rows[0].astype(jnp.float32)
    summed = summed + (
        partial_value.reshape(token_count, breadth // QB, QB) * factor[None, :, None]
    ).reshape(token_count, breadth)
    return summed


def body(master_weight, gradient, first_moment, second_moment, hidden, owner_of_expert, slab_order):
    updated, moment_one, moment_two = adam_step(
        master_weight, gradient, first_moment, second_moment
    )
    quantized, block_scale = quantize(updated)
    experts = quantized.shape[0]
    slab_rows = quantized.shape[1]
    places = jnp.arange(experts, dtype=jnp.int32)
    held_expert = jnp.sum(
        jnp.where(owner_of_expert[None, :] == places[:, None], places[None, :], 0), axis=1
    )
    outgoing = jnp.take(quantized, held_expert, axis=0)
    outgoing_scale = jnp.take(block_scale, held_expert, axis=0)
    tokens = hidden.shape[2]
    token_rows = hidden.reshape(tokens, hidden.shape[3])
    replica_count = slab_order.shape[0]
    position = jnp.arange(replica_count, dtype=jnp.int32)
    zero_sum = jnp.zeros((tokens, D), jnp.float32)
    copies_quant, copies_scale = (
        lax.all_gather(outgoing[None], "replica", axis=0, tiled=True),
        lax.all_gather(outgoing_scale[None], "replica", axis=0, tiled=True),
    )
    own_quant, own_scale = (
        lax.all_to_all(copies_quant, "shard", split_axis=1, concat_axis=3, tiled=True),
        lax.all_to_all(copies_scale, "shard", split_axis=1, concat_axis=3, tiled=True),
    )
    quant_piece = own_quant[:, 0]
    scale_piece = own_scale[:, 0]

    def one_slab(offset, current):
        replica = 0 + offset
        chosen = jnp.sum(jnp.where(position == replica, slab_order, 0))
        left_part = lax.dynamic_slice_in_dim(token_rows, chosen * slab_rows, slab_rows, 1)
        slab_quant = lax.dynamic_index_in_dim(quant_piece, offset, 0, keepdims=False)
        slab_scale = lax.dynamic_index_in_dim(scale_piece, offset, 0, keepdims=False)
        return scaled_product(current, left_part, slab_quant, slab_scale)

    summed = lax.fori_loop(0, quant_piece.shape[0], one_slab, zero_sum)
    expert_out = summed.astype(jnp.bfloat16).reshape(1, 1, tokens, D)
    return (updated, moment_one.astype(jnp.bfloat16), moment_two.astype(jnp.bfloat16), expert_out)


def solution(mesh):
    placed = (
        P(None, "replica", "shard"),
        P(None, "replica", "shard"),
        P(None, "replica", "shard"),
        P(None, "replica", "shard"),
        P("replica", "shard", None, None),
        P(),
        P(),
    )
    return jax.shard_map(
        body,
        mesh=mesh,
        in_specs=placed,
        out_specs=(
            P(None, "replica", "shard"),
            P(None, "replica", "shard"),
            P(None, "replica", "shard"),
            P("replica", "shard", None, None),
        ),
        check_vma=False,
    )
```

profile of v0, /device:TPU:1, one launch (start us, length us, event | category | flops | bytes accessed | tf_op | source)
XLA Modules:
  0.0 441.6 jit_solution(2416194118943100054)
XLA Ops:
  8.0 5.8 %abs_reduce_fusion = (f32[32]{0:T(128)S(1)}, f32[32,128,128]{2,1,0:T(8,128)S(1)}, bf16[32,128,128]{2,1,0:T(8,128)(2,1)}, bf16[32,128,128]{2,1,0:T(8,128)(2,1)}) fusion(f32[32,128,128]{2,1,0:T(8,128)} %param.9, bf16[32,128,128]{2,1,0:T(8,128)(2,1)} %param.12, bf16[32,128,128]{2,1,0:T(8,128)(2,1)} %param.10, bf16[32,128,128]{2,1,0:T(8,128)(2,1)} %param.11), kind=kLoop, calls=%fused_computation.20 | loop fusion | flops 10485728 | bytes 9437312 | tf_op jit(solution)/shard_map/reduce_max | solution.py:35
  15.4 2.0 gather_fusion
  19.3 20.6 %all_gather.7 = bf16[8,32,1,1]{1,3,2,0:T(2,128)(2,1)S(1)} all-gather(bf16[1,32,1,1]{1,3,2,0:T(2,128)(2,1)S(1)} %and_select_fusion), channel_id=1, replica_groups=mesh['replica'=8,'shard'=32] {'replica'}, dimensions={0}, use_global_device_ids=true | all-gather | bytes 576 | tf_op jit(solution)/shard_map/all_gather | solution.py:73
  40.6 13.2 %all-to-all-start.1 = ((bf16[8,32,1,1]{0,3,2,1:T(2,128)(2,1)}), bf16[8,32,1,1]{0,3,2,1:T(2,128)(2,1)S(1)}, u32[]{:S(2)}, u32[]{:S(2)}) async-start(bf16[8,32,1,1]{0,3,2,1:T(2,128)(2,1)} %copy.32), calls=%async_computation.1 | async-start | bytes 32768 | tf_op jit(solution)/shard_map/all_to_all | solution.py:77
  53.8 79.5 %all-gather.2.cloned.1.call-done = bf16[8,32,128,128]{3,2,1,0:T(8,128)(2,1)} async-done(((bf16[1,32,128,128]{3,2,1,0:T(8,128)(2,1)}), bf16[8,32,128,128]{3,2,1,0:T(8,128)(2,1)}) %all-gather.2.cloned.1.call-update) | async-done | bytes 8388624 | tf_op jit(solution)/shard_map/all_gather | solution.py:72
  133.3 10.3 %copy.30 = bf16[8,32,128,128]{3,2,0,1:T(8,128)(2,1)} copy(bf16[8,32,128,128]{3,2,1,0:T(8,128)(2,1)} %all-gather.2.cloned.1.call-done) | data formatting | bytes 16777216 | tf_op jit(solution)/shard_map/all_gather | solution.py:72
  143.7 8.6 %all-to-all-start = ((bf16[8,32,128,128]{3,2,0,1:T(8,128)(2,1)}), bf16[8,32,128,128]{3,2,0,1:T(8,128)(2,1)}, u32[]{:S(2)}, u32[]{:S(2)}) async-start(bf16[8,32,128,128]{3,2,0,1:T(8,128)(2,1)} %copy.30), calls=%async_computation | async-start | bytes 16777216 | tf_op jit(solution)/shard_map/all_to_all | solution.py:76
  152.4 186.4 %all-to-all-done = bf16[8,32,128,128]{3,2,0,1:T(8,128)(2,1)} async-done(((bf16[8,32,128,128]{3,2,0,1:T(8,128)(2,1)}), bf16[8,32,128,128]{3,2,0,1:T(8,128)(2,1)}, u32[]{:S(2)}, u32[]{:S(2)}) %all-to-all-start) | async-done | bytes 8388640 | tf_op jit(solution)/shard_map/all_to_all | solution.py:76
  338.8 12.0 %copy.31 = bf16[8,32,128,128]{2,3,1,0:T(8,128)(2,1)} copy(bf16[8,32,128,128]{3,2,0,1:T(8,128)(2,1)} %all-to-all-done) | data formatting | bytes 16777216 | tf_op jit(solution)/shard_map/all_to_all | solution.py:76
  350.8 78.6 %while.14 = (s32[]{:T(128)}, f32[384,4096]{0,1:T(8,128)}, s32[8]{0:T(128)S(1)}, bf16[384,1024]{1,0:T(8,128)(2,1)}, bf16[8,128,4096]{1,2,0:T(8,128)(2,1)}, /*inde...) while((s32[]{:T(128)}, f32[384,4096]{0,1:T(8,128)}, ...), condition=%wide.region_4.5_spmd.clone, body=%wide.region_2.4_spmd.clone.sunk | while | flops 407371840 | bytes 78742096 | solution.py:90
  353.5 2.0 broadcast_multiply_fusion.2
  356.3 1.6 bitcast_add_fusion.2
  357.9 2.6 copy-done.1
  363.3 2.0 broadcast_multiply_fusion.2
  366.1 1.6 bitcast_add_fusion.2
  367.8 2.6 copy-done.1
  373.1 2.0 broadcast_multiply_fusion.2
  376.0 1.6 bitcast_add_fusion.2
  377.6 2.6 copy-done.1
  382.9 2.0 broadcast_multiply_fusion.2
  387.4 2.6 copy-done.1
  392.8 2.0 broadcast_multiply_fusion.2
  395.6 1.6 bitcast_add_fusion.2
  397.2 2.6 copy-done.1
  402.6 2.0 broadcast_multiply_fusion.2
  407.1 2.6 copy-done.1
  412.4 2.0 broadcast_multiply_fusion.2
  415.2 1.6 bitcast_add_fusion.2
  416.9 2.6 copy-done.1
  422.2 2.0 broadcast_multiply_fusion.2
  426.7 2.6 copy-done.1
  429.4 5.4 %copy.35 = bf16[384,4096]{1,0:T(8,128)(2,1)} copy(f32[384,4096]{0,1:T(8,128)} %get-tuple-element.128) | data formatting | bytes 9437184 | tf_op jit(solution)/shard_map/while | solution.py:90
  (71 shorter events, 32.3 us)
Async XLA Ops:
  7.2 126.2 %all-gather.2.cloned.1.call-start = ((), (), s32[]{:S(2)}) async-start(), calls=%async_computation.2 | async-start | bytes 9437184 | tf_op jit(solution)/shard_map/all_gather | solution.py:72
  13.8 3.6 copy-start.2
  40.6 103.1 %all-to-all-start.1 = ((bf16[8,32,1,1]{0,3,2,1:T(2,128)(2,1)}), bf16[8,32,1,1]{0,3,2,1:T(2,128)(2,1)S(1)}, u32[]{:S(2)}, u32[]{:S(2)}) async-start(bf16[8,32,1,1]{0,3,2,1:T(2,128)(2,1)} %copy.32), calls=%async_computation.1 | async-start | bytes 32768 | tf_op jit(solution)/shard_map/all_to_all | solution.py:77
  143.7 195.1 %all-to-all-start = ((bf16[8,32,128,128]{3,2,0,1:T(8,128)(2,1)}), bf16[8,32,128,128]{3,2,0,1:T(8,128)(2,1)}, u32[]{:S(2)}, u32[]{:S(2)}) async-start(bf16[8,32,128,128]{3,2,0,1:T(8,128)(2,1)} %copy.30), calls=%async_computation | async-start | bytes 16777216 | tf_op jit(solution)/shard_map/all_to_all | solution.py:76
  152.4 198.4 %copy-start.3 = (s32[8]{0:T(128)S(1)}, s32[8]{0:T(128)}, u32[]{:S(2)}) copy-start(s32[8]{0:T(128)} %param.15) | copy-start | bytes 100
  353.5 2.8 copy-start
  357.9 2.7 copy-start.1
  363.3 2.8 copy-start
  367.8 2.7 copy-start.1
  373.1 2.8 copy-start
  377.6 2.7 copy-start.1
  382.9 2.8 copy-start
  387.4 2.7 copy-start.1
  392.8 2.8 copy-start
  397.2 2.7 copy-start.1
  402.6 2.8 copy-start
  407.1 2.7 copy-start.1
  412.4 2.8 copy-start
  416.9 2.7 copy-start.1
  422.2 2.8 copy-start
  426.7 2.7 copy-start.1
Sparse Core Ops, SparseCore 0:
  18.7 114.6 all-gather.1
where the time goes:
time: 443 us; the launch traced here: 442 us
  waiting for transfers between devices  266 us (60%)
  local copies, waits for them, and re-layouts  68.9 us (16%)
  other arithmetic  28 us (6%)
  starting transfers between devices  21.9 us (5%)
  blocking collectives  20.6 us (5%)
  matrix products  16.3 us (4%)
  between operations  14.1 us (3%)
  loops' own time  5.84 us (1%)
    all_to_all x1, waiting for transfers between devices, body(): lax.all_to_all(copies_quant, 'shard', split_axis=1, concat_axis=3, tiled=...  186 us
    all_gather x1, waiting for transfers between devices, body(): lax.all_gather(outgoing[None], 'replica', axis=0, tiled=True)  79.5 us
    while x32, local copies, waits for them, and re-layouts  27.4 us
    all_gather x1, blocking collectives, body(): lax.all_gather(outgoing_scale[None], 'replica', axis=0, tiled=True)  20.6 us
    dot_general x8, matrix products, scaled_product(): jnp.dot(left_part, quant_rows, preferred_element_type=jnp.float32)  16.3 us
    all_to_all x1, starting transfers between devices, body(): lax.all_to_all(copies_scale, 'shard', split_axis=1, concat_axis=3, tiled=...  13.2 us
    add x8, other arithmetic, scaled_product(): summed + (partial_value.reshape(token_count, breadth // QB, QB) * factor[...  13 us
    all_to_all x1, local copies, waits for them, and re-layouts, body(): lax.all_to_all(copies_quant, 'shard', split_axis=1, concat_axis=3, tiled=...  12 us
  transfers between devices with their start and end apart: 3, of which 2 were waited for; matrix products, arithmetic and copies ran while one was open for 3% of the time, Pallas kernels for 0%

commit v1 on v0

v1 whole, which is shorter than its diff:
```python
import functools

import jax
import jax.numpy as jnp
from jax import lax
from jax.experimental import pallas as pl
from jax.experimental.pallas import tpu as pltpu
from jax.sharding import PartitionSpec as P

D = 4096
FFW = 1024
QB = 128
TOK = 384
EXPERTS = 32
REPLICAS = 8
ZS = 8
GROUP = 4

beta_one = 0.9
beta_two = 0.95
learn_rate = 0.004
adam_epsilon = 1e-08
step_count = 10.0
quant_limit = 448.0
scale_epsilon = 1e-06
first_fix = 1.0 - beta_one**step_count
second_fix = 1.0 - beta_two**step_count

MESH = pl.DeviceIdType.MESH
ADAM_STEP = 8


def adam_kernel(
    owner_ref, slab_ref, w_ref, g_ref, m_ref, v_ref, ha_ref, hb_ref, nw_ref, nm_ref, nv_ref, out_ref, ho_ref
):
    step = pl.program_id(0)
    ho_ref[:, :QB] = ha_ref[...]
    ho_ref[:, QB:] = hb_ref[...]
    for i in range(ADAM_STEP):
        g = g_ref[i].astype(jnp.float32)
        first = beta_one * m_ref[i].astype(jnp.float32) + (1.0 - beta_one) * g
        second = beta_two * v_ref[i].astype(jnp.float32) + (1.0 - beta_two) * g * g
        update = first / first_fix / (jnp.sqrt(second / second_fix) + adam_epsilon)
        w = w_ref[i] - learn_rate * update
        nw_ref[i] = w
        nm_ref[i] = first.astype(jnp.bfloat16)
        nv_ref[i] = second.astype(jnp.bfloat16)
        largest = jnp.max(jnp.abs(w), axis=(0, 1), keepdims=True)
        scale = ((largest + scale_epsilon) / quant_limit).astype(jnp.bfloat16).astype(jnp.float32)
        quantized = (w * (1.0 / scale)).astype(jnp.bfloat16).astype(jnp.float32)
        out_ref[owner_ref[step * ADAM_STEP + i]] = (quantized * scale).astype(jnp.bfloat16)


def adam(owner, slab, w, g, m, v, hidden):
    block = pl.BlockSpec((ADAM_STEP, QB, QB), lambda e, o, p: (e, 0, 0))
    whole = pl.BlockSpec((EXPERTS, QB, QB), lambda e, o, p: (0, 0, 0))
    even = pl.BlockSpec((TOK, QB), lambda e, o, p: (0, p[2 * e]))
    odd = pl.BlockSpec((TOK, QB), lambda e, o, p: (0, p[2 * e + 1]))
    pair = pl.BlockSpec((TOK, 2 * QB), lambda e, o, p: (0, e))
    shape = (EXPERTS, QB, QB)
    return pl.pallas_call(
        adam_kernel,
        out_shape=(
            jax.ShapeDtypeStruct(shape, jnp.float32),
            jax.ShapeDtypeStruct(shape, jnp.bfloat16),
            jax.ShapeDtypeStruct(shape, jnp.bfloat16),
            jax.ShapeDtypeStruct(shape, jnp.bfloat16),
            jax.ShapeDtypeStruct((TOK, FFW), jnp.bfloat16),
        ),
        grid_spec=pltpu.PrefetchScalarGridSpec(
            num_scalar_prefetch=2,
            grid=(EXPERTS // ADAM_STEP,),
            in_specs=[block] * 4 + [even, odd],
            out_specs=(block, block, block, whole, pair),
        ),
        compiler_params=pltpu.CompilerParams(
            dimension_semantics=("arbitrary",), vmem_limit_bytes=24 * 2**20
        ),
        name="adam_quantize",
    )(owner, slab, w, g, m, v, hidden, hidden)


ORDER = (0, 1, 7, 2, 6, 3, 5, 4)
SPLIT = ((3, 2, 0), (2, 1, 1), (3, 1, 1), (2, 1, 1)) * 2


def deliver_kernel(mine, ordered, out, full, obuf, asem, ssem, rsem, osem, lsem):
    r, s = lax.axis_index("replica"), lax.axis_index("shard")
    xh, y = r // 4, r % 4
    z, xl, c = s // 4, (s // 2) % 2, s % 2
    xo = 1 - xh
    up, down, far = (y + 1) % 4, (y + 3) % 4, (y + 2) % 4

    def peer(dz, dx, dc):
        return ((z + dz) % ZS) * 4 + ((xl + dx) % 2) * 2 + (c + dc) % 2

    others = [(dx, dc) for dx in range(2) for dc in range(2)]
    exchange = [(i, dx, dc) for i in range(ZS) for dx, dc in others if (ORDER[i], dx, dc) != (0, 0, 0)]

    barrier = pltpu.get_barrier_semaphore()
    for i, dx, dc in exchange:
        pl.semaphore_signal(barrier, inc=1, device_id=(r, peer(ORDER[i], dx, dc)), device_id_type=MESH)
    for there in ((xh * 4 + up, s), (xh * 4 + down, s), (xo * 4 + y, s)):
        pl.semaphore_signal(barrier, inc=1, device_id=there, device_id_type=MESH)
    pl.semaphore_wait(barrier, len(exchange) + 3)

    own = pltpu.make_async_copy(mine.at[s], full.at[r, s], lsem)
    own.start()
    first = []
    for n, (i, dx, dc) in enumerate(exchange):
        p = peer(ORDER[i], dx, dc)
        copy = pltpu.make_async_remote_copy(
            mine.at[p], full.at[r, s], asem.at[0, n], asem.at[1, n], device_id=(r, p), device_id_type=MESH
        )
        copy.start()
        first.append(copy)

    pending = []
    serial = {}

    def send(group, kind, row, begin, count, there):
        at = serial.setdefault((group, kind), len(serial))
        tiles = full.at[row, pl.ds(begin, count)]
        copy = pltpu.make_async_remote_copy(
            tiles, tiles, ssem.at[at], rsem.at[at], device_id=there, device_id_type=MESH
        )
        copy.start()
        pending.append(copy)

    def arrive(group, kind, row, begin, count):
        at = serial[(group, kind)]
        tiles = full.at[row, pl.ds(begin, count)]
        pltpu.make_async_remote_copy(
            tiles, tiles, ssem.at[at], rsem.at[at], device_id=(r, s), device_id_type=MESH
        ).wait_recv()

    def base_of(i):
        return ((z + ORDER[i]) % ZS) * GROUP

    def at_row(hi, yy):
        return hi * 4 + yy

    to_up, to_down, to_x = (xh * 4 + up, s), (xh * 4 + down, s), (xo * 4 + y, s)

    def stage0(i):
        base = base_of(i)
        if i == 0:
            own.wait()
        for n, (k, dx, dc) in enumerate(exchange):
            if k == i:
                src = peer(ORDER[i], dx, dc)
                pltpu.make_async_remote_copy(
                    mine.at[0], full.at[r, src], asem.at[0, n], asem.at[1, recv_slot(n)], device_id=(r, s),
                    device_id_type=MESH,
                ).wait_recv()
        np_, hp, hq = SPLIT[i]
        nq = GROUP - np_
        send(i, "px", r, base, np_, to_x)
        send(i, "py+", r, base, np_, to_up)
        send(i, "py-", r, base, np_, to_down)
        send(i, "qy+", r, base + np_, nq, to_up)
        send(i, "qy-", r, base + np_, nq, to_down)
        send(i, "qx0", r, base + np_, nq, to_x)

    def recv_slot(n):
        i, dx, dc = exchange[n]
        mirrored = (ORDER.index((ZS - ORDER[i]) % ZS), dx, dc)
        return exchange.index(mirrored)

    def stage1(i):
        base = base_of(i)
        np_, hp, hq = SPLIT[i]
        nq = GROUP - np_
        qb = base + np_
        arrive(i, "px", at_row(xo, y), base, np_)
        send(i, "xy+", at_row(xo, y), base, np_, to_up)
        send(i, "xy-", at_row(xo, y), base, np_, to_down)
        arrive(i, "py+", at_row(xh, down), base, np_)
        send(i, "pf+", at_row(xh, down), base, hp, to_up)
        arrive(i, "py-", at_row(xh, up), base, np_)
        send(i, "pf-", at_row(xh, up), base + hp, np_ - hp, to_down)
        arrive(i, "qy+", at_row(xh, down), qb, nq)
        if hq:
            send(i, "qf+", at_row(xh, down), qb, hq, to_up)
        send(i, "qx1", at_row(xh, down), qb, nq, to_x)
        arrive(i, "qy-", at_row(xh, up), qb, nq)
        if nq - hq:
            send(i, "qf-", at_row(xh, up), qb + hq, nq - hq, to_down)
        send(i, "qx2", at_row(xh, up), qb, nq, to_x)

    def stage2(i):
        base = base_of(i)
        np_, hp, hq = SPLIT[i]
        nq = GROUP - np_
        qb = base + np_
        arrive(i, "xy+", at_row(xo, down), base, np_)
        send(i, "xf+", at_row(xo, down), base, hp, to_up)
        arrive(i, "xy-", at_row(xo, up), base, np_)
        send(i, "xf-", at_row(xo, up), base + hp, np_ - hp, to_down)
        if hq:
            arrive(i, "qf+", at_row(xh, far), qb, hq)
        if nq - hq:
            arrive(i, "qf-", at_row(xh, far), qb + hq, nq - hq)
        send(i, "qx3", at_row(xh, far), qb, nq, to_x)

    writes = [None, None]

    def stage3(i):
        base = base_of(i)
        np_, hp, hq = SPLIT[i]
        nq = GROUP - np_
        qb = base + np_
        arrive(i, "pf+", at_row(xh, far), base, hp)
        arrive(i, "pf-", at_row(xh, far), base + hp, np_ - hp)
        arrive(i, "qx0", at_row(xo, y), qb, nq)
        arrive(i, "qx1", at_row(xo, down), qb, nq)
        arrive(i, "qx2", at_row(xo, up), qb, nq)
        arrive(i, "xf+", at_row(xo, far), base, hp)
        arrive(i, "xf-", at_row(xo, far), base + hp, np_ - hp)
        arrive(i, "qx3", at_row(xo, far), qb, nq)
        slot = i % 2
        if writes[slot] is not None:
            writes[slot].wait()
        for half in range(2):
            right = jnp.concatenate(
                [full[:, base + half * 2 + k].reshape(FFW, QB) for k in range(2)], axis=1
            )
            value = jnp.dot(ordered[...], right, preferred_element_type=jnp.float32)
            obuf[slot, :, half * 2 * QB:(half + 1) * 2 * QB] = value.astype(jnp.bfloat16)
        columns = pl.ds(pl.multiple_of(base * QB, GROUP * QB), GROUP * QB)
        writes[slot] = pltpu.make_async_copy(obuf.at[slot], out.at[:, columns], osem.at[slot])
        writes[slot].start()

    stages = (stage0, stage1, stage2, stage3)
    for t in range(ZS + len(stages) - 1):
        for lag, stage in enumerate(stages):
            if 0 <= t - lag < ZS:
                stage(t - lag)
    for copy in first:
        copy.wait_send()
    for copy in pending:
        copy.wait_send()
    for write in writes:
        write.wait()


def deliver(mine, ordered):
    copies = 17 * ZS
    return pl.pallas_call(
        deliver_kernel,
        out_shape=jax.ShapeDtypeStruct((TOK, D), jnp.bfloat16),
        in_specs=[
            pl.BlockSpec(memory_space=pltpu.VMEM),
            pl.BlockSpec(memory_space=pltpu.VMEM),
        ],
        out_specs=pl.BlockSpec(memory_space=pl.ANY),
        scratch_shapes=[
            pltpu.VMEM((REPLICAS, EXPERTS, QB, QB), jnp.bfloat16),
            pltpu.VMEM((2, TOK, GROUP * QB), jnp.bfloat16),
            pltpu.SemaphoreType.DMA((2, EXPERTS - 1)),
            pltpu.SemaphoreType.DMA((copies,)),
            pltpu.SemaphoreType.DMA((copies,)),
            pltpu.SemaphoreType.DMA((2,)),
            pltpu.SemaphoreType.DMA,
        ],
        compiler_params=pltpu.CompilerParams(
            collective_id=0, has_side_effects=True, vmem_limit_bytes=40 * 2**20
        ),
        name="deliver",
    )(mine, ordered)


def body(master_weight, gradient, first_moment, second_moment, hidden, owner_of_expert, slab_order):
    updated, moment_one, moment_two, outgoing, ordered = adam(
        owner_of_expert, slab_order, master_weight, gradient, first_moment, second_moment, hidden.reshape(TOK, FFW)
    )
    expert_out = deliver(outgoing, ordered)
    return updated, moment_one, moment_two, expert_out.reshape(1, 1, TOK, D)


def solution(mesh):
    learner = P(None, "replica", "shard")
    rollout = P("replica", "shard", None, None)
    return jax.shard_map(
        body,
        mesh=mesh,
        in_specs=(learner, learner, learner, learner, rollout, P(), P()),
        out_specs=(learner, learner, learner, rollout),
        check_vma=False,
    )
```

time: 443 us -> 94.9 us (0.21)
  waiting for transfers between devices: 266 us -> 0 us
  Pallas kernels: 0 us -> 84.6 us
  local copies, waits for them, and re-layouts: 68.9 us -> 9.37 us
  other arithmetic: 28 us -> 0 us
  starting transfers between devices: 21.9 us -> 0 us
  blocking collectives: 20.6 us -> 0 us
  matrix products: 16.3 us -> 0 us
  between operations: 14.1 us -> 0.66 us
  loops' own time: 5.84 us -> 0 us
    all_to_all x2 -> x0, waiting for transfers between devices: 186 us -> none  [the longest x1 186 us: body(): lax.all_to_all(copies_quant, 'shard', split_axis=1, concat_axis=3, tiled=...]
    pallas_call x0 -> x2, Pallas kernels: none -> 84.6 us  [the longest x1 80.1 us: deliver(): pl.pallas_call(deliver_kernel, out_shape=jax.ShapeDtypeStruct((TOK, D), j...]
    all_gather x1 -> x0, waiting for transfers between devices: 79.5 us -> none  [body(): lax.all_gather(outgoing[None], 'replica', axis=0, tiled=True)]
    while x33 -> x0, local copies, waits for them, and re-layouts: 32.8 us -> none
    all_to_all x2 -> x0, starting transfers between devices: 21.8 us -> none  [the longest x1 13.2 us: body(): lax.all_to_all(copies_scale, 'shard', split_axis=1, concat_axis=3, tiled=...]
    all_gather x1 -> x0, blocking collectives: 20.6 us -> none  [body(): lax.all_gather(outgoing_scale[None], 'replica', axis=0, tiled=True)]
    dot_general x8 -> x0, matrix products: 16.3 us -> none  [scaled_product(): jnp.dot(left_part, quant_rows, preferred_element_type=jnp.float32)]
    add x8 -> x0, other arithmetic: 13 us -> none  [scaled_product(): summed + (partial_value.reshape(token_count, breadth // QB, QB) * factor[...]
  transfers between devices with their start and end apart: 3 -> 0, of which waited for: 2 -> 0; matrix products, arithmetic and copies ran while one was open for 3% -> 0% of each run, Pallas kernels for 0% -> 0%
where the time goes in v1:
time: 94.9 us; the launch traced here: 94.6 us
  Pallas kernels  84.6 us (89%)
  local copies, waits for them, and re-layouts  9.37 us (10%)
    pallas_call x1, Pallas kernels, deliver(): pl.pallas_call(deliver_kernel, out_shape=jax.ShapeDtypeStruct((TOK, D), j...  80.1 us
    unnamed x15, local copies, waits for them, and re-layouts  9.37 us
    pallas_call x1, Pallas kernels, adam(): pl.pallas_call(adam_kernel, out_shape=(jax.ShapeDtypeStruct(shape, jnp.fl...  4.44 us

profile of v1, /device:TPU:1, one launch (start us, length us, event | category | flops | bytes accessed | tf_op | source)
XLA Modules:
  0.0 94.6 jit_solution(237581636859890425)
XLA Ops:
  0.6 0.0 copy-start
  0.6 1.1 %copy-done = bf16[1,1,384,1024]{3,2,1,0:T(8,128)(2,1)S(1)} copy-done((bf16[1,1,384,1024]{3,2,1,0:T(8,128)(2,1)S(1)}, bf16[1,1,384,1024]{3,2,1,0:T(8,128)(2,1)}, u32[]{:S(2)}) %copy-start) | copy-done | bytes 786456
  1.8 0.0 copy-start.1
  1.8 1.6 %copy-done.1 = f32[32,128,128]{2,1,0:T(8,128)S(1)} copy-done((f32[32,128,128]{2,1,0:T(8,128)S(1)}, f32[32,128,128]{2,1,0:T(8,128)}, u32[]{:S(2)}) %copy-start.1) | copy-done | bytes 2097176
  3.4 0.0 copy-start.2
  3.4 1.2 %copy-done.2 = bf16[32,128,128]{2,1,0:T(8,128)(2,1)S(1)} copy-done((bf16[32,128,128]{2,1,0:T(8,128)(2,1)S(1)}, bf16[32,128,128]{2,1,0:T(8,128)(2,1)}, u32[]{:S(2)}) %copy-start.2) | copy-done | bytes 1048600
  4.6 0.0 copy-start.3
  4.6 1.2 %copy-done.3 = bf16[32,128,128]{2,1,0:T(8,128)(2,1)S(1)} copy-done((bf16[32,128,128]{2,1,0:T(8,128)(2,1)S(1)}, bf16[32,128,128]{2,1,0:T(8,128)(2,1)}, u32[]{:S(2)}) %copy-start.3) | copy-done | bytes 1048600
  5.8 0.0 copy-start.4
  5.8 1.2 %copy-done.4 = bf16[32,128,128]{2,1,0:T(8,128)(2,1)S(1)} copy-done((bf16[32,128,128]{2,1,0:T(8,128)(2,1)S(1)}, bf16[32,128,128]{2,1,0:T(8,128)(2,1)}, u32[]{:S(2)}) %copy-start.4) | copy-done | bytes 1048600
  7.0 0.0 copy-start.5
  7.0 0.7 copy-done.5
  7.7 0.0 copy-start.6
  7.7 0.7 copy-done.6
  8.3 4.4 %adam_quantize.1 = (f32[32,128,128]{2,1,0:T(8,128)}, bf16[32,128,128]{2,1,0:T(8,128)(2,1)}, bf16[32,128,128]{2,1,0:T(8,128)(2,1)}, bf16[32,128,128]{2,1,0:T(8,128)(2,1)S(1)}, bf16[384,1024]{1,0:T(8,128)(2,1)S(1)}) custom-call(s32[32]{0:T(128)S(1)} %copy-done.5, s32[8]{0:T(128)S(1)} %copy-done.6, f32[32,128,128]{2,1,0:T(8,128)S(1)} %copy-done.1, ...), custom_call_target="tpu_custom_call" | custom-call | tf_op jit(solution)/shard_map/adam_quantize/pallas_call | solution.py:61
  12.8 80.1 %deliver.1 = bf16[384,4096]{1,0:T(8,128)(2,1)S(1)} custom-call(bf16[32,128,128]{2,1,0:T(8,128)(2,1)S(1)} %get-tuple-element.12.mine, bf16[384,1024]{1,0:T(8,128)(2,1)S(1)} %get-tuple-element.13.ordered), custom_call_target="tpu_custom_call" | custom-call | tf_op jit(solution)/shard_map/deliver/pallas_call | solution.py:249
  92.9 1.7 %copy.12 = bf16[1,1,384,4096]{3,2,1,0:T(8,128)(2,1)} copy(bf16[1,1,384,4096]{3,2,1,0:T(8,128)(2,1)S(1)} %bitcast.2) | data formatting | bytes 6291456
Async XLA Ops:
  0.6 1.1 %copy-start = (bf16[1,1,384,1024]{3,2,1,0:T(8,128)(2,1)S(1)}, bf16[1,1,384,1024]{3,2,1,0:T(8,128)(2,1)}, u32[]{:S(2)}) copy-start(bf16[1,1,384,1024]{3,2,1,0:T(8,128)(2,1)} %param.11) | copy-start | bytes 2359300
  1.8 1.6 %copy-start.1 = (f32[32,128,128]{2,1,0:T(8,128)S(1)}, f32[32,128,128]{2,1,0:T(8,128)}, u32[]{:S(2)}) copy-start(f32[32,128,128]{2,1,0:T(8,128)} %w_ref.1) | copy-start | bytes 6291460
  3.4 1.2 %copy-start.2 = (bf16[32,128,128]{2,1,0:T(8,128)(2,1)S(1)}, bf16[32,128,128]{2,1,0:T(8,128)(2,1)}, u32[]{:S(2)}) copy-start(bf16[32,128,128]{2,1,0:T(8,128)(2,1)} %g_ref.1) | copy-start | bytes 3145732
  4.6 1.2 %copy-start.3 = (bf16[32,128,128]{2,1,0:T(8,128)(2,1)S(1)}, bf16[32,128,128]{2,1,0:T(8,128)(2,1)}, u32[]{:S(2)}) copy-start(bf16[32,128,128]{2,1,0:T(8,128)(2,1)} %m_ref.1) | copy-start | bytes 3145732
  5.8 1.2 %copy-start.4 = (bf16[32,128,128]{2,1,0:T(8,128)(2,1)S(1)}, bf16[32,128,128]{2,1,0:T(8,128)(2,1)}, u32[]{:S(2)}) copy-start(bf16[32,128,128]{2,1,0:T(8,128)(2,1)} %v_ref.1) | copy-start | bytes 3145732
  7.0 0.7 copy-start.5
  7.7 0.7 copy-start.6

commit v2 on v0

v2 whole, which is shorter than its diff:
```python
import functools

import jax
import jax.numpy as jnp
from jax import lax
from jax.experimental import pallas as pl
from jax.experimental.pallas import tpu as pltpu
from jax.sharding import PartitionSpec as P

D = 4096
FFW = 1024
QB = 128
TOK = 384
EXPERTS = 32
REPLICAS = 8
ZS = 8

beta_one = 0.9
beta_two = 0.95
learn_rate = 0.004
adam_epsilon = 1e-08
step_count = 10.0
quant_limit = 448.0
scale_epsilon = 1e-06
first_fix = 1.0 - beta_one**step_count
second_fix = 1.0 - beta_two**step_count

MESH = pl.DeviceIdType.MESH
CHUNK = 4
CHUNKS = EXPERTS // CHUNK


def adam_kernel(
    owner, slab, w_hbm, g_hbm, m_hbm, v_hbm, hidden, nw_hbm, nm_hbm, nv_hbm, mine, ordered,
    w_in, g_in, m_in, v_in, w_out, m_out, v_out, in_sem, out_sem, slab_sem,
):
    def loads(k):
        part = pl.ds(k * CHUNK, CHUNK)
        return [
            pltpu.make_async_copy(hbm.at[part], vmem.at[part], in_sem.at[j, k])
            for j, (hbm, vmem) in enumerate(((g_hbm, g_in), (m_hbm, m_in), (v_hbm, v_in), (w_hbm, w_in)))
        ]

    def stores(k):
        part = pl.ds(k * CHUNK, CHUNK)
        return [
            pltpu.make_async_copy(vmem.at[part], hbm.at[part], out_sem.at[j, k])
            for j, (vmem, hbm) in enumerate(((w_out, nw_hbm), (m_out, nm_hbm), (v_out, nv_hbm)))
        ]

    xh = lax.axis_index("replica") // 4
    xl = (lax.axis_index("shard") // 2) % 2

    def place_of(e):
        to = owner[e]
        return (to // 4) * 4 + (to % 2) * 2 + (to // 2 + xl) % 2

    for k in range(CHUNKS):
        for copy in loads(k):
            copy.start()
    slabs = []
    for j in range(REPLICAS):
        begin = pl.multiple_of(slab[(xh * 4 + j) % REPLICAS] * QB, QB)
        slabs.append(
            pltpu.make_async_copy(hidden.at[:, pl.ds(begin, QB)], ordered.at[:, pl.ds(j * QB, QB)], slab_sem.at[j])
        )
        slabs[j].start()

    @pl.loop(0, CHUNKS)
    def _(k):
        for copy in loads(k):
            copy.wait()
        for i in range(CHUNK):
            e = k * CHUNK + i
            g = g_in[e].astype(jnp.float32)
            first = beta_one * m_in[e].astype(jnp.float32) + (1.0 - beta_one) * g
            second = beta_two * v_in[e].astype(jnp.float32) + (1.0 - beta_two) * g * g
            update = (learn_rate / first_fix) * first / (jnp.sqrt(second * (1.0 / second_fix)) + adam_epsilon)
            w = w_in[e] - update
            w_out[e] = w
            m_out[e] = first.astype(jnp.bfloat16)
            v_out[e] = second.astype(jnp.bfloat16)
            largest = jnp.max(jnp.abs(w), axis=(0, 1), keepdims=True)
            scale = ((largest + scale_epsilon) / quant_limit).astype(jnp.bfloat16).astype(jnp.float32)
            quantized = (w * (1.0 / scale)).astype(jnp.bfloat16).astype(jnp.float32)
            mine[place_of(e)] = (quantized * scale).astype(jnp.bfloat16)
        for copy in stores(k):
            copy.start()

    for copy in slabs:
        copy.wait()
    for k in range(CHUNKS):
        for copy in stores(k):
            copy.wait()


def adam(owner, slab, w, g, m, v, hidden):
    shape = (EXPERTS, QB, QB)
    hbm = pl.BlockSpec(memory_space=pltpu.HBM)
    smem = pl.BlockSpec(memory_space=pltpu.SMEM)
    vmem = pl.BlockSpec(memory_space=pltpu.VMEM)
    f32, bf16 = jnp.float32, jnp.bfloat16
    return pl.pallas_call(
        adam_kernel,
        out_shape=(
            jax.ShapeDtypeStruct(shape, f32),
            jax.ShapeDtypeStruct(shape, bf16),
            jax.ShapeDtypeStruct(shape, bf16),
            jax.ShapeDtypeStruct(shape, bf16),
            jax.ShapeDtypeStruct((TOK, FFW), bf16),
        ),
        in_specs=[smem, smem, hbm, hbm, hbm, hbm, hbm],
        out_specs=(hbm, hbm, hbm, vmem, vmem),
        scratch_shapes=[pltpu.VMEM(shape, t) for t in (f32, bf16, bf16, bf16, f32, bf16, bf16)]
        + [
            pltpu.SemaphoreType.DMA((4, CHUNKS)),
            pltpu.SemaphoreType.DMA((3, CHUNKS)),
            pltpu.SemaphoreType.DMA((REPLICAS,)),
        ],
        compiler_params=pltpu.CompilerParams(vmem_limit_bytes=52500 * 1024),
        name="adam_quantize",
    )(owner, slab, w, g, m, v, hidden)


ORDER = (0, 1, 7, 2, 6, 3, 5, 4)
LAGS = (1, 2, 3)


def deliver_kernel(mine, ordered, out, spread, same, cross, both, obuf, asem, ssem, rsem, lsem):
    r, s = lax.axis_index("replica"), lax.axis_index("shard")
    xh, y = r // 4, r % 4
    z, xl, c = s // 4, (s // 2) % 2, s % 2
    up, down, far = (y + 1) % 4, (y + 3) % 4, (y + 2) % 4
    role = (y + c) % 2
    partner = (y + 1 + 2 * role) % 4

    def owner_at(zz, cc):
        return zz * 4 + xl * 2 + cc

    exchange = [(i, dc) for i in range(ZS) for dc in range(2) if (ORDER[i], dc) != (0, 0)]
    to_up, to_down, to_far = ((xh * 4 + place, s) for place in (up, down, far))
    to_partner = (xh * 4 + partner, s)
    beside = z * 4 + (1 - xl) * 2 + c
    to_two, to_near, to_cross = ((1 - xh) * 4 + y, s), (r, beside), ((1 - xh) * 4 + y, beside)

    barrier = pltpu.get_barrier_semaphore()
    for i, dc in exchange:
        there = (r, owner_at((z + ORDER[i]) % ZS, (c + dc) % 2))
        pl.semaphore_signal(barrier, inc=1, device_id=there, device_id_type=MESH)
    for there in (to_up, to_down, to_far, to_two, to_near, to_cross):
        pl.semaphore_signal(barrier, inc=1, device_id=there, device_id_type=MESH)
    pl.semaphore_wait(barrier, len(exchange) + 6)

    pending = []
    serial = {}

    def send(key, src, dst, there):
        at = serial.setdefault(key, len(serial))
        copy = pltpu.make_async_remote_copy(
            src, dst, ssem.at[at], rsem.at[at], device_id=there, device_id_type=MESH
        )
        copy.start()
        pending.append(copy)

    def arrive(key, dst):
        at = serial[key]
        pltpu.make_async_remote_copy(
            dst, dst, ssem.at[at], rsem.at[at], device_id=(r, s), device_id_type=MESH
        ).wait_recv()

    own = pltpu.make_async_copy(mine.at[pl.ds(z * 4 + c * 2, 2)], spread.at[y, z, c], lsem.at[0])
    own.start()
    keep = pltpu.make_async_copy(ordered, both.at[pl.ds(0, TOK)], lsem.at[1])
    keep.start()
    theirs = both.at[pl.ds(TOK, TOK)]
    first = []
    for n, (i, dc) in enumerate(exchange):
        zz, cc = (z + ORDER[i]) % ZS, (c + dc) % 2
        copy = pltpu.make_async_remote_copy(
            mine.at[pl.ds(zz * 4 + cc * 2, 2)], spread.at[y, z, c], asem.at[0, n], asem.at[1, n],
            device_id=(r, owner_at(zz, cc)), device_id_type=MESH,
        )
        copy.start()
        first.append(copy)
        if n == 0:
            send("hidden", ordered, theirs, to_partner)

    def recv_slot(n):
        i, dc = exchange[n]
        return exchange.index((ORDER.index((ZS - ORDER[i]) % ZS), dc))

    def send_x(i, name, place):
        zz = (z + ORDER[i]) % ZS
        tile, other = spread.at[place, zz, role, 0], spread.at[place, zz, role, 1]
        send((i, name, "two"), tile, same.at[place, zz], to_two)
        send((i, name, "near"), other, cross.at[0, place, zz], to_near)
        send((i, name, "cross"), other, cross.at[1, place, zz], to_cross)

    def stage0(i):
        zz = (z + ORDER[i]) % ZS
        if i == 0:
            own.wait()
        for n, (k, dc) in enumerate(exchange):
            if k == i:
                got = spread.at[y, zz, (c + dc) % 2]
                pltpu.make_async_remote_copy(
                    got, got, asem.at[0, n], asem.at[1, recv_slot(n)], device_id=(r, s), device_id_type=MESH
                ).wait_recv()
        given, used = spread.at[y, zz, 1 - role], spread.at[y, zz, role]
        send_x(i, "own", y)
        send((i, "up"), given, given, to_up)
        send((i, "down"), given, given, to_down)
        send((i, "far"), used, used, to_far)

    def stage1(i):
        for name, place in (("up", down), ("down", up), ("far", far)):
            arrive((i, name), spread.at[place, (z + ORDER[i]) % ZS, role])
            send_x(i, name, place)

    def stage2(i):
        zz = (z + ORDER[i]) % ZS
        for name, place in (("own", y), ("up", down), ("down", up), ("far", far)):
            arrive((i, name, "two"), same.at[place, zz])
            arrive((i, name, "near"), cross.at[0, place, zz])
            arrive((i, name, "cross"), cross.at[1, place, zz])
        if i == 0:
            keep.wait()
            arrive("hidden", theirs)
        half = FFW // 2
        right = jnp.concatenate(
            [
                jnp.concatenate([spread[:, zz, role, 0].reshape(half, QB), same[:, zz].reshape(half, QB)], axis=0),
                cross[:, :, zz].reshape(FFW, QB),
            ],
            axis=1,
        )
        for whose in (1, 0):
            left = both[whose * TOK:(whose + 1) * TOK]
            value = jnp.dot(left, right, preferred_element_type=jnp.float32).astype(jnp.bfloat16)
            for k in range(2):
                part = value[:, k * QB:(k + 1) * QB]
                if whose:
                    obuf[i, k] = part
                else:
                    out[:, columns(i, k, role)] = part

    def columns(i, k, q):
        zz = (z + ORDER[i]) % ZS
        return pl.ds(pl.multiple_of((zz * 4 + ((xl + k) % 2) * 2 + q) * QB, QB), QB)

    def stage3(i):
        for k in range(2):
            send((i, "out", k), obuf.at[i, k], out.at[:, columns(i, k, role)], to_partner)

    stages = ((0, stage0), (LAGS[0], stage1), (LAGS[1], stage2), (LAGS[2], stage3))
    for t in range(ZS + LAGS[2]):
        for lag, stage in stages:
            if 0 <= t - lag < ZS:
                stage(t - lag)
    for i in range(ZS):
        for k in range(2):
            arrive((i, "out", k), out.at[:, columns(i, k, 1 - role)])
    for copy in first:
        copy.wait_send()
    for copy in pending:
        copy.wait_send()


def deliver(mine, ordered):
    copies = 17 * ZS + 1
    bf16 = jnp.bfloat16
    return pl.pallas_call(
        deliver_kernel,
        out_shape=jax.ShapeDtypeStruct((TOK, D), bf16),
        in_specs=[pl.BlockSpec(memory_space=pltpu.VMEM)] * 2,
        out_specs=pl.BlockSpec(memory_space=pltpu.VMEM),
        scratch_shapes=[
            pltpu.VMEM((4, ZS, 2, 2, QB, QB), bf16),
            pltpu.VMEM((4, ZS, QB, QB), bf16),
            pltpu.VMEM((2, 4, ZS, QB, QB), bf16),
            pltpu.VMEM((2 * TOK, FFW), bf16),
            pltpu.VMEM((ZS, 2, TOK, QB), bf16),
            pltpu.SemaphoreType.DMA((2, 2 * ZS - 1)),
            pltpu.SemaphoreType.DMA((copies,)),
            pltpu.SemaphoreType.DMA((copies,)),
            pltpu.SemaphoreType.DMA((2,)),
        ],
        compiler_params=pltpu.CompilerParams(
            collective_id=0, has_side_effects=True, vmem_limit_bytes=24 * 2**20
        ),
        name="deliver",
    )(mine, ordered)


def body(master_weight, gradient, first_moment, second_moment, hidden, owner_of_expert, slab_order):
    updated, moment_one, moment_two, outgoing, ordered = adam(
        owner_of_expert, slab_order, master_weight, gradient, first_moment, second_moment, hidden.reshape(TOK, FFW)
    )
    expert_out = deliver(outgoing, ordered)
    return updated, moment_one, moment_two, expert_out.reshape(1, 1, TOK, D)


def solution(mesh):
    learner = P(None, "replica", "shard")
    rollout = P("replica", "shard", None, None)
    return jax.shard_map(
        body,
        mesh=mesh,
        in_specs=(learner, learner, learner, learner, rollout, P(), P()),
        out_specs=(learner, learner, learner, rollout),
        check_vma=False,
    )
```

time: 443 us -> 89.2 us (0.20)
  waiting for transfers between devices: 266 us -> 0 us
  Pallas kernels: 0 us -> 83.4 us
  local copies, waits for them, and re-layouts: 68.9 us -> 4.1 us
  other arithmetic: 28 us -> 0 us
  starting transfers between devices: 21.9 us -> 0 us
  blocking collectives: 20.6 us -> 0 us
  matrix products: 16.3 us -> 0 us
  between operations: 14.1 us -> 0.66 us
  loops' own time: 5.84 us -> 0 us
    all_to_all x2 -> x0, waiting for transfers between devices: 186 us -> none  [the longest x1 186 us: body(): lax.all_to_all(copies_quant, 'shard', split_axis=1, concat_axis=3, tiled=...]
    pallas_call x0 -> x2, Pallas kernels: none -> 83.4 us  [the longest x1 77.3 us: deliver(): pl.pallas_call(deliver_kernel, out_shape=jax.ShapeDtypeStruct((TOK, D), b...]
    all_gather x1 -> x0, waiting for transfers between devices: 79.5 us -> none  [body(): lax.all_gather(outgoing[None], 'replica', axis=0, tiled=True)]
    while x33 -> x0, local copies, waits for them, and re-layouts: 32.8 us -> none
    all_to_all x2 -> x0, starting transfers between devices: 21.8 us -> none  [the longest x1 13.2 us: body(): lax.all_to_all(copies_scale, 'shard', split_axis=1, concat_axis=3, tiled=...]
    all_gather x1 -> x0, blocking collectives: 20.6 us -> none  [body(): lax.all_gather(outgoing_scale[None], 'replica', axis=0, tiled=True)]
    dot_general x8 -> x0, matrix products: 16.3 us -> none  [scaled_product(): jnp.dot(left_part, quant_rows, preferred_element_type=jnp.float32)]
    add x8 -> x0, other arithmetic: 13 us -> none  [scaled_product(): summed + (partial_value.reshape(token_count, breadth // QB, QB) * factor[...]
  transfers between devices with their start and end apart: 3 -> 0, of which waited for: 2 -> 0; matrix products, arithmetic and copies ran while one was open for 3% -> 0% of each run, Pallas kernels for 0% -> 0%
where the time goes in v2:
time: 89.2 us; the launch traced here: 88.1 us
  Pallas kernels  83.4 us (93%)
  local copies, waits for them, and re-layouts  4.1 us (5%)
    pallas_call x1, Pallas kernels, deliver(): pl.pallas_call(deliver_kernel, out_shape=jax.ShapeDtypeStruct((TOK, D), b...  77.3 us
    pallas_call x1, Pallas kernels, adam(): pl.pallas_call(adam_kernel, out_shape=(jax.ShapeDtypeStruct(shape, f32),...  6.07 us
    unnamed x7, local copies, waits for them, and re-layouts  4.1 us

profile of v2, /device:TPU:1, one launch (start us, length us, event | category | flops | bytes accessed | tf_op | source)
XLA Modules:
  0.0 88.1 jit_solution(15287670692928564001)
XLA Ops:
  0.6 0.0 copy-start
  0.6 1.1 %copy-done = bf16[1,1,384,1024]{3,2,1,0:T(8,128)(2,1)S(1)} copy-done((bf16[1,1,384,1024]{3,2,1,0:T(8,128)(2,1)S(1)}, bf16[1,1,384,1024]{3,2,1,0:T(8,128)(2,1)}, u32[]{:S(2)}) %copy-start) | copy-done | bytes 786456
  1.8 0.0 copy-start.1
  1.8 0.7 copy-done.1
  2.4 0.0 copy-start.2
  2.4 0.7 copy-done.2
  3.1 6.1 %adam_quantize.1 = (f32[32,128,128]{2,1,0:T(8,128)}, bf16[32,128,128]{2,1,0:T(8,128)(2,1)}, bf16[32,128,128]{2,1,0:T(8,128)(2,1)}, bf16[32,128,128]{2,1,0:T(8,128)(2,1)S(1)}, bf16[384,1024]{1,0:T(8,128)(2,1)S(1)}) custom-call(s32[32]{0:T(128)S(1)} %copy-done.1, s32[8]{0:T(128)S(1)} %copy-done.2, f32[32,128,128]{2,1,0:T(8,128)} %w_hbm.1, ...), custom_call_target="tpu_custom_call" | custom-call | tf_op jit(solution)/shard_map/adam_quantize/pallas_call | solution.py:103
  9.2 77.3 %deliver.1 = bf16[384,4096]{1,0:T(8,128)(2,1)S(1)} custom-call(bf16[32,128,128]{2,1,0:T(8,128)(2,1)S(1)} %get-tuple-element.12.mine, bf16[384,1024]{1,0:T(8,128)(2,1)S(1)} %get-tuple-element.13.ordered), custom_call_target="tpu_custom_call" | custom-call | tf_op jit(solution)/shard_map/deliver/pallas_call | solution.py:272
  86.5 1.7 %copy.12 = bf16[1,1,384,4096]{3,2,1,0:T(8,128)(2,1)} copy(bf16[1,1,384,4096]{3,2,1,0:T(8,128)(2,1)S(1)} %bitcast.2) | data formatting | bytes 6291456
Async XLA Ops:
  0.6 1.1 %copy-start = (bf16[1,1,384,1024]{3,2,1,0:T(8,128)(2,1)S(1)}, bf16[1,1,384,1024]{3,2,1,0:T(8,128)(2,1)}, u32[]{:S(2)}) copy-start(bf16[1,1,384,1024]{3,2,1,0:T(8,128)(2,1)} %param.11) | copy-start | bytes 2359300
  1.8 0.7 copy-start.1
  2.4 0.7 copy-start.2

commit v3 on v2

--- a/solution.py
+++ b/solution.py
@@ -31,8 +31,8 @@
 
 
 def adam_kernel(
-    owner, slab, w_hbm, g_hbm, m_hbm, v_hbm, hidden, nw_hbm, nm_hbm, nv_hbm, mine, ordered,
-    w_in, g_in, m_in, v_in, w_out, m_out, v_out, in_sem, out_sem, slab_sem,
+    owner, w_hbm, g_hbm, m_hbm, v_hbm, nw_hbm, nm_hbm, nv_hbm, mine,
+    w_in, g_in, m_in, v_in, w_out, m_out, v_out, in_sem, out_sem,
 ):
     def loads(k):
         part = pl.ds(k * CHUNK, CHUNK)
@@ -48,7 +48,6 @@
             for j, (vmem, hbm) in enumerate(((w_out, nw_hbm), (m_out, nm_hbm), (v_out, nv_hbm)))
         ]
 
-    xh = lax.axis_index("replica") // 4
     xl = (lax.axis_index("shard") // 2) % 2
 
     def place_of(e):
@@ -58,13 +57,6 @@
     for k in range(CHUNKS):
         for copy in loads(k):
             copy.start()
-    slabs = []
-    for j in range(REPLICAS):
-        begin = pl.multiple_of(slab[(xh * 4 + j) % REPLICAS] * QB, QB)
-        slabs.append(
-            pltpu.make_async_copy(hidden.at[:, pl.ds(begin, QB)], ordered.at[:, pl.ds(j * QB, QB)], slab_sem.at[j])
-        )
-        slabs[j].start()
 
     @pl.loop(0, CHUNKS)
     def _(k):
@@ -87,14 +79,12 @@
         for copy in stores(k):
             copy.start()
 
-    for copy in slabs:
-        copy.wait()
     for k in range(CHUNKS):
         for copy in stores(k):
             copy.wait()
 
 
-def adam(owner, slab, w, g, m, v, hidden):
+def adam(owner, w, g, m, v):
     shape = (EXPERTS, QB, QB)
     hbm = pl.BlockSpec(memory_space=pltpu.HBM)
     smem = pl.BlockSpec(memory_space=pltpu.SMEM)
@@ -107,26 +97,28 @@
             jax.ShapeDtypeStruct(shape, bf16),
             jax.ShapeDtypeStruct(shape, bf16),
             jax.ShapeDtypeStruct(shape, bf16),
-            jax.ShapeDtypeStruct((TOK, FFW), bf16),
         ),
-        in_specs=[smem, smem, hbm, hbm, hbm, hbm, hbm],
-        out_specs=(hbm, hbm, hbm, vmem, vmem),
+        in_specs=[smem, hbm, hbm, hbm, hbm],
+        out_specs=(hbm, hbm, hbm, vmem),
         scratch_shapes=[pltpu.VMEM(shape, t) for t in (f32, bf16, bf16, bf16, f32, bf16, bf16)]
         + [
             pltpu.SemaphoreType.DMA((4, CHUNKS)),
             pltpu.SemaphoreType.DMA((3, CHUNKS)),
-            pltpu.SemaphoreType.DMA((REPLICAS,)),
         ],
-        compiler_params=pltpu.CompilerParams(vmem_limit_bytes=52500 * 1024),
+        compiler_params=pltpu.CompilerParams(vmem_limit_bytes=53400 * 1024),
         name="adam_quantize",
-    )(owner, slab, w, g, m, v, hidden)
+    )(owner, w, g, m, v)
 
 
 ORDER = (0, 1, 7, 2, 6, 3, 5, 4)
-LAGS = (1, 2, 3)
-
-
-def deliver_kernel(mine, ordered, out, spread, same, cross, both, obuf, asem, ssem, rsem, lsem):
+LAGS = (2, 5, 6)
+SWAP = 2
+FIRST_X = (1, 3, 5)
+
+
+def deliver_kernel(
+    slab, mine, hidden, out, spread, same, cross, passing, held, theirs, both, obuf, asem, ssem, rsem, lsem
+):
     r, s = lax.axis_index("replica"), lax.axis_index("shard")
     xh, y = r // 4, r % 4
     z, xl, c = s // 4, (s // 2) % 2, s % 2
@@ -170,9 +162,10 @@
 
     own = pltpu.make_async_copy(mine.at[pl.ds(z * 4 + c * 2, 2)], spread.at[y, z, c], lsem.at[0])
     own.start()
-    keep = pltpu.make_async_copy(ordered, both.at[pl.ds(0, TOK)], lsem.at[1])
-    keep.start()
-    theirs = both.at[pl.ds(TOK, TOK)]
+    keep = []
+    for j in range(REPLICAS):
+        keep.append(pltpu.make_async_copy(hidden.at[:, pl.ds(j * QB, QB)], held.at[j], lsem.at[1 + j]))
+        keep[j].start()
     first = []
     for n, (i, dc) in enumerate(exchange):
         zz, cc = (z + ORDER[i]) % ZS, (c + dc) % 2
@@ -182,8 +175,6 @@
         )
         copy.start()
         first.append(copy)
-        if n == 0:
-            send("hidden", ordered, theirs, to_partner)
 
     def recv_slot(n):
         i, dc = exchange[n]
@@ -193,6 +184,8 @@
         zz = (z + ORDER[i]) % ZS
         tile, other = spread.at[place, zz, role, 0], spread.at[place, zz, role, 1]
         send((i, name, "two"), tile, same.at[place, zz], to_two)
+        if i in FIRST_X and name != "own":
+            return
         send((i, name, "near"), other, cross.at[0, place, zz], to_near)
         send((i, name, "cross"), other, cross.at[1, place, zz], to_cross)
 
@@ -208,24 +201,46 @@
                 ).wait_recv()
         given, used = spread.at[y, zz, 1 - role], spread.at[y, zz, role]
         send_x(i, "own", y)
+        if i in FIRST_X:
+            given, used = spread.at[y, zz, 1 - role, 0], spread.at[y, zz, role, 0]
+            other = spread.at[y, zz, 1 - role, 1]
+            for side, there in enumerate((to_near, to_cross)):
+                send((i, "pass", side), other, passing.at[side, FIRST_X.index(i)], there)
         send((i, "up"), given, given, to_up)
         send((i, "down"), given, given, to_down)
         send((i, "far"), used, used, to_far)
 
     def stage1(i):
+        zz = (z + ORDER[i]) % ZS
         for name, place in (("up", down), ("down", up), ("far", far)):
-            arrive((i, name), spread.at[place, (z + ORDER[i]) % ZS, role])
+            got = spread.at[place, zz, role, 0] if i in FIRST_X else spread.at[place, zz, role]
+            arrive((i, name), got)
             send_x(i, name, place)
+        if i in FIRST_X:
+            for side, name in enumerate(("near", "cross")):
+                used, other = cross.at[side, y, zz], passing.at[side, FIRST_X.index(i)]
+                arrive((i, "own", name), used)
+                send((i, "far", side), used, used, to_far)
+                arrive((i, "pass", side), other)
+                send((i, "up", side), other, used, to_up)
+                send((i, "down", side), other, used, to_down)
 
     def stage2(i):
         zz = (z + ORDER[i]) % ZS
         for name, place in (("own", y), ("up", down), ("down", up), ("far", far)):
             arrive((i, name, "two"), same.at[place, zz])
-            arrive((i, name, "near"), cross.at[0, place, zz])
-            arrive((i, name, "cross"), cross.at[1, place, zz])
+            if i not in FIRST_X:
+                arrive((i, name, "near"), cross.at[0, place, zz])
+                arrive((i, name, "cross"), cross.at[1, place, zz])
+            elif name != "own":
+                for side in range(2):
+                    arrive((i, name, side), cross.at[side, place, zz])
         if i == 0:
-            keep.wait()
-            arrive("hidden", theirs)
+            for j in range(REPLICAS):
+                arrive(("slab", j), theirs.at[j])
+            for whose, slabs in enumerate((held, theirs)):
+                for j in range(REPLICAS):
+                    both[whose * TOK:(whose + 1) * TOK, j * QB:(j + 1) * QB] = slabs[slab[(xh * 4 + j) % REPLICAS]]
         half = FFW // 2
         right = jnp.concatenate(
             [
@@ -252,11 +267,18 @@
         for k in range(2):
             send((i, "out", k), obuf.at[i, k], out.at[:, columns(i, k, role)], to_partner)
 
+    def swap_slabs(t):
+        for j in range(t * SWAP, (t + 1) * SWAP):
+            keep[j].wait()
+            send(("slab", j), held.at[j], theirs.at[j], to_partner)
+
     stages = ((0, stage0), (LAGS[0], stage1), (LAGS[1], stage2), (LAGS[2], stage3))
     for t in range(ZS + LAGS[2]):
         for lag, stage in stages:
             if 0 <= t - lag < ZS:
                 stage(t - lag)
+            if stage is stage1 and t * SWAP < REPLICAS:
+                swap_slabs(t)
     for i in range(ZS):
         for k in range(2):
             arrive((i, "out", k), out.at[:, columns(i, k, 1 - role)])
@@ -266,37 +288,44 @@
         copy.wait_send()
 
 
-def deliver(mine, ordered):
-    copies = 17 * ZS + 1
+def deliver(slab, mine, hidden):
+    copies = 20 * ZS
     bf16 = jnp.bfloat16
     return pl.pallas_call(
         deliver_kernel,
         out_shape=jax.ShapeDtypeStruct((TOK, D), bf16),
-        in_specs=[pl.BlockSpec(memory_space=pltpu.VMEM)] * 2,
+        in_specs=[
+            pl.BlockSpec(memory_space=pltpu.SMEM),
+            pl.BlockSpec(memory_space=pltpu.VMEM),
+            pl.BlockSpec(memory_space=pl.ANY),
+        ],
         out_specs=pl.BlockSpec(memory_space=pltpu.VMEM),
         scratch_shapes=[
             pltpu.VMEM((4, ZS, 2, 2, QB, QB), bf16),
             pltpu.VMEM((4, ZS, QB, QB), bf16),
             pltpu.VMEM((2, 4, ZS, QB, QB), bf16),
+            pltpu.VMEM((2, max(len(FIRST_X), 1), QB, QB), bf16),
+            pltpu.VMEM((REPLICAS, TOK, QB), bf16),
+            pltpu.VMEM((REPLICAS, TOK, QB), bf16),
             pltpu.VMEM((2 * TOK, FFW), bf16),
             pltpu.VMEM((ZS, 2, TOK, QB), bf16),
             pltpu.SemaphoreType.DMA((2, 2 * ZS - 1)),
             pltpu.SemaphoreType.DMA((copies,)),
             pltpu.SemaphoreType.DMA((copies,)),
-            pltpu.SemaphoreType.DMA((2,)),
+            pltpu.SemaphoreType.DMA((1 + REPLICAS,)),
         ],
         compiler_params=pltpu.CompilerParams(
             collective_id=0, has_side_effects=True, vmem_limit_bytes=24 * 2**20
         ),
         name="deliver",
-    )(mine, ordered)
+    )(slab, mine, hidden)
 
 
 def body(master_weight, gradient, first_moment, second_moment, hidden, owner_of_expert, slab_order):
-    updated, moment_one, moment_two, outgoing, ordered = adam(
-        owner_of_expert, slab_order, master_weight, gradient, first_moment, second_moment, hidden.reshape(TOK, FFW)
+    updated, moment_one, moment_two, outgoing = adam(
+        owner_of_expert, master_weight, gradient, first_moment, second_moment
     )
-    expert_out = deliver(outgoing, ordered)
+    expert_out = deliver(slab_order, outgoing, hidden.reshape(TOK, FFW))
     return updated, moment_one, moment_two, expert_out.reshape(1, 1, TOK, D)
 
 

time: 89.2 us -> 78.9 us (0.88); the launches traced: 88.1 us -> 78.8 us
  Pallas kernels: 83.4 us -> 75.7 us
  local copies, waits for them, and re-layouts: 4.1 us -> 2.4 us
    pallas_call x1, Pallas kernels: 77.3 us -> 69.7 us  [deliver(): pl.pallas_call(deliver_kernel, out_shape=jax.ShapeDtypeStruct((TOK, D), b...]
    unnamed x7, local copies, waits for them, and re-layouts: 4.1 us -> 2.4 us
where the time goes in v3:
time: 78.9 us; the launch traced here: 78.8 us
  Pallas kernels  75.7 us (96%)
  local copies, waits for them, and re-layouts  2.4 us (3%)
    pallas_call x1, Pallas kernels, deliver(): pl.pallas_call(deliver_kernel, out_shape=jax.ShapeDtypeStruct((TOK, D), b...  69.7 us
    pallas_call x1, Pallas kernels, adam(): pl.pallas_call(adam_kernel, out_shape=(jax.ShapeDtypeStruct(shape, f32),...  6 us
    unnamed x7, local copies, waits for them, and re-layouts  2.4 us

profile of v3, /device:TPU:1, one launch (start us, length us, event | category | flops | bytes accessed | tf_op | source)
XLA Modules:
  0.0 78.8 jit_solution(7928957178438740372)
XLA Ops:
  0.6 0.0 copy-start.1
  0.6 0.0 copy-start
  0.7 0.0 copy-start.2
  0.7 0.7 copy-done.2
  1.4 6.0 %adam_quantize.1 = (f32[32,128,128]{2,1,0:T(8,128)}, bf16[32,128,128]{2,1,0:T(8,128)(2,1)}, bf16[32,128,128]{2,1,0:T(8,128)(2,1)}, bf16[32,128,128]{2,1,0:T(8,128)(2,1)S(1)}) custom-call(s32[32]{0:T(128)S(1)} %copy-done.2, f32[32,128,128]{2,1,0:T(8,128)} %w_hbm.1, bf16[32,128,128]{2,1,0:T(8,128)(2,1)} %g_hbm.1, bf16[32,128,128]{2,1,0:T(8,128)(2,1)} %m_hbm.1, ...), custom_call_target="tpu_custom_call" | custom-call | tf_op jit(solution)/shard_map/adam_quantize/pallas_call | solution.py:93
  7.4 0.0 copy-done.1
  7.4 0.0 copy-done
  7.4 69.7 %deliver.1 = bf16[384,4096]{1,0:T(8,128)(2,1)S(1)} custom-call(s32[8]{0:T(128)S(1)} %copy-done.1, bf16[32,128,128]{2,1,0:T(8,128)(2,1)S(1)} %get-tuple-element.11.mine, bf16[384,1024]{1,0:T(8,128)(2,1)S(1)} %bitcast.3), custom_call_target="tpu_custom_call" | custom-call | tf_op jit(solution)/shard_map/deliver/pallas_call | solution.py:294
  77.1 1.7 %copy.12 = bf16[1,1,384,4096]{3,2,1,0:T(8,128)(2,1)} copy(bf16[1,1,384,4096]{3,2,1,0:T(8,128)(2,1)S(1)} %bitcast.2) | data formatting | bytes 6291456
Async XLA Ops:
  0.6 6.8 %copy-start.1 = (s32[8]{0:T(128)S(1)}, s32[8]{0:T(128)}, u32[]{:S(2)}) copy-start(s32[8]{0:T(128)} %slab.1) | copy-start | bytes 100
  0.6 6.8 %copy-start = (bf16[1,1,384,1024]{3,2,1,0:T(8,128)(2,1)S(1)}, bf16[1,1,384,1024]{3,2,1,0:T(8,128)(2,1)}, u32[]{:S(2)}) copy-start(bf16[1,1,384,1024]{3,2,1,0:T(8,128)(2,1)} %param.11) | copy-start | bytes 2359300
  0.7 0.7 copy-start.2

commit v4 on v3

--- a/solution.py
+++ b/solution.py
@@ -26,7 +26,7 @@
 second_fix = 1.0 - beta_two**step_count
 
 MESH = pl.DeviceIdType.MESH
-CHUNK = 4
+CHUNK = 8
 CHUNKS = EXPERTS // CHUNK
 
 

time: 78.9 us -> 78.2 us (level)
  no operation moved by 1% of the time
where the time goes in v4:
time: 78.2 us; the launch traced here: 78.1 us
  Pallas kernels  75 us (96%)
  local copies, waits for them, and re-layouts  2.4 us (3%)
    pallas_call x1, Pallas kernels, deliver(): pl.pallas_call(deliver_kernel, out_shape=jax.ShapeDtypeStruct((TOK, D), b...  69.7 us
    pallas_call x1, Pallas kernels, adam(): pl.pallas_call(adam_kernel, out_shape=(jax.ShapeDtypeStruct(shape, f32),...  5.34 us
    unnamed x7, local copies, waits for them, and re-layouts  2.4 us

profile of v4, /device:TPU:1, one launch (start us, length us, event | category | flops | bytes accessed | tf_op | source)
XLA Modules:
  0.0 78.1 jit_solution(10255898956543526413)
XLA Ops:
  0.6 0.0 copy-start.1
  0.6 0.0 copy-start
  0.7 0.0 copy-start.2
  0.7 0.7 copy-done.2
  1.4 5.3 %adam_quantize.1 = (f32[32,128,128]{2,1,0:T(8,128)}, bf16[32,128,128]{2,1,0:T(8,128)(2,1)}, bf16[32,128,128]{2,1,0:T(8,128)(2,1)}, bf16[32,128,128]{2,1,0:T(8,128)(2,1)S(1)}) custom-call(s32[32]{0:T(128)S(1)} %copy-done.2, f32[32,128,128]{2,1,0:T(8,128)} %w_hbm.1, bf16[32,128,128]{2,1,0:T(8,128)(2,1)} %g_hbm.1, bf16[32,128,128]{2,1,0:T(8,128)(2,1)} %m_hbm.1, ...), custom_call_target="tpu_custom_call" | custom-call | tf_op jit(solution)/shard_map/adam_quantize/pallas_call | solution.py:93
  6.7 0.0 copy-done.1
  6.7 0.0 copy-done
  6.7 69.7 %deliver.1 = bf16[384,4096]{1,0:T(8,128)(2,1)S(1)} custom-call(s32[8]{0:T(128)S(1)} %copy-done.1, bf16[32,128,128]{2,1,0:T(8,128)(2,1)S(1)} %get-tuple-element.11.mine, bf16[384,1024]{1,0:T(8,128)(2,1)S(1)} %bitcast.3), custom_call_target="tpu_custom_call" | custom-call | tf_op jit(solution)/shard_map/deliver/pallas_call | solution.py:294
  76.4 1.7 %copy.12 = bf16[1,1,384,4096]{3,2,1,0:T(8,128)(2,1)} copy(bf16[1,1,384,4096]{3,2,1,0:T(8,128)(2,1)S(1)} %bitcast.2) | data formatting | bytes 6291456
Async XLA Ops:
  0.6 6.1 %copy-start.1 = (s32[8]{0:T(128)S(1)}, s32[8]{0:T(128)}, u32[]{:S(2)}) copy-start(s32[8]{0:T(128)} %slab.1) | copy-start | bytes 100
  0.6 6.1 %copy-start = (bf16[1,1,384,1024]{3,2,1,0:T(8,128)(2,1)S(1)}, bf16[1,1,384,1024]{3,2,1,0:T(8,128)(2,1)}, u32[]{:S(2)}) copy-start(bf16[1,1,384,1024]{3,2,1,0:T(8,128)(2,1)} %param.11) | copy-start | bytes 2359300
  0.7 0.7 copy-start.2
